TPU v7x, 32 devices: a whole 2x2x4 slice. The times are simulated.
32 devices in a mesh: grp: 4 (over y, core), row: 8 (over z, x).
Axes of the slice: x: 2, y: 2, z: 4, core: 2. Of those that a mesh axis runs over, the one named last changes fastest.
Arguments:
- landmarks: bfloat16 [1024, 1024], P(('grp', 'row')), may hold values from -6.5 to 6.5
- initial_basis: bfloat16 [1024, 256], P(('grp', 'row')), may hold values from -0.1875 to 0.1875
- points: bfloat16 [32768, 1024], P(('grp', 'row')), may hold values from -6.5 to 6.5
Outputs:
- basis: float32 [1024, 256], P(('grp', 'row'))
- coords: float32 [32768, 256], P(('grp', 'row'))
All inputs are finite; a program needn't handle non-finite values.
Results may differ from a plain program's by a relative error of at most 0.0057.
Values may be sent and summed in bfloat16 or wider, within the bound.
No kernel may reach another device: no remote copies, remote signals or barrier semaphores. Data moves between devices by JAX's collectives and lax.ppermute only.
A program may use at most 128 MiB of HBM per device.

v0:
```python
import math
import jax
import jax.numpy as jnp
from jax import lax
from jax.sharding import PartitionSpec as P

ITERS = 2
spread = 0.25


def squared_rows(rows):
    return jnp.sum(jnp.square(rows.astype(jnp.float32)), axis=1)


def pair_kernel(left, right):
    inner = lax.dot_general(
        left, right, (((1,), (1,)), ((), ())), preferred_element_type=jnp.float32
    )
    dist = squared_rows(left)[:, None] + squared_rows(right)[None, :] - 2.0 * inner
    return jnp.exp(-dist / (spread * left.shape[1]))


def point_terms(anchors, spectral_rows, members, member_sq):
    inner = lax.dot_general(
        anchors, members, (((1,), (1,)), ((), ())), preferred_element_type=jnp.float32
    )
    dist = squared_rows(anchors)[:, None] + member_sq[None, :] - 2.0 * inner
    kernel_part = jnp.exp(-dist / (spread * anchors.shape[1]))
    degree_part = jnp.sum(kernel_part, axis=0)
    numer_part = lax.dot_general(
        kernel_part.astype(jnp.bfloat16),
        spectral_rows,
        (((0,), (0,)), ((), ())),
        preferred_element_type=jnp.float32,
    )
    return (numer_part, degree_part)


def body(landmarks, initial_basis, points):
    local_rows = landmarks.shape[0]
    total = local_rows * lax.axis_size("grp") * lax.axis_size("row")
    row_index = lax.axis_index("row")
    group_rows = lax.all_gather(landmarks, "row", axis=0, tiled=True)
    cross_rows = lax.all_gather(landmarks, "grp", axis=0, tiled=True)
    land_kernel = pair_kernel(group_rows, cross_rows)
    group_degree = lax.psum(jnp.sum(land_kernel, axis=1), "row")
    own_degree = lax.dynamic_slice_in_dim(group_degree, row_index * local_rows, local_rows, 0)
    cross_degree = lax.psum(jnp.sum(land_kernel, axis=0), "grp")
    row_scale = 1.0 / jnp.sqrt(group_degree)
    column_scale = 1.0 / jnp.sqrt(cross_degree)
    affinity = (land_kernel * row_scale[:, None] * column_scale[None, :]).astype(jnp.bfloat16)
    current = initial_basis
    for step in range(ITERS):
        cross_basis = lax.all_gather(current, "grp", axis=0, tiled=True)
        image = lax.psum_scatter(
            jnp.dot(affinity, cross_basis, preferred_element_type=jnp.float32),
            "row",
            scatter_dimension=0,
            tiled=True,
        )
        gram = lax.psum(jnp.dot(image.T, image, precision=lax.Precision.HIGHEST), ("grp", "row"))
        lower = jnp.linalg.cholesky(gram)
        ortho = jax.scipy.linalg.solve_triangular(lower, image.T, lower=True).T
        current = ortho.astype(jnp.bfloat16)
    lam = jnp.diagonal(lower)
    own_scale = 1.0 / jnp.sqrt(own_degree)
    spectral = (ortho * own_scale[:, None] / lam[None, :]).astype(jnp.bfloat16)
    point_sq = squared_rows(points)
    numer_part, degree_part = point_terms(
        lax.all_gather(landmarks, ("grp", "row"), axis=0, tiled=True),
        lax.all_gather(spectral, ("grp", "row"), axis=0, tiled=True),
        points,
        point_sq,
    )
    coords = numer_part / jnp.sqrt(degree_part)[:, None] * math.sqrt(total)
    return (ortho, coords)


def solution(mesh):
    in_specs = (P(("grp", "row"), None), P(("grp", "row"), None), P(("grp", "row"), None))
    out_specs = (P(("grp", "row"), None), P(("grp", "row"), None))
    return jax.shard_map(body, mesh=mesh, in_specs=in_specs, out_specs=out_specs, check_vma=False)
```

profile of v0, /device:TPU:0, one launch (start us, length us, event | category | flops | bytes accessed | tf_op | source)
XLA Modules:
  0.0 683.4 jit_solution(5649184369802876398)
XLA Ops:
  7.2 7.5 %all_gather.19 = bf16[128,1024]{1,0:T(8,128)(2,1)S(1)} all-gather(bf16[32,1024]{1,0:T(8,128)(2,1)} %param.6), channel_id=1, replica_groups=mesh['grp'=4,'row'=8] {'grp'}, dimensions={0}, use_global_device_ids=true | all-gather | bytes 327680 | tf_op jit(solution)/shard_map/all_gather | solution.py:44
  14.7 32.1 %all_gather.18 = bf16[256,1024]{1,0:T(8,128)(2,1)S(1)} all-gather(bf16[32,1024]{1,0:T(8,128)(2,1)} %param.6), channel_id=1, replica_groups=mesh['grp'=4,'row'=8] {'row'}, dimensions={0}, use_global_device_ids=true | all-gather | bytes 589824 | tf_op jit(solution)/shard_map/all_gather | solution.py:43
  46.7 5.4 all_gather.20
  52.5 0.4 fusion.37
  52.9 21.4 %psum.28 = f32[256]{0:T(256)S(1)} all-reduce(f32[256]{0:T(256)S(1)} %get-tuple-element.20), channel_id=1, replica_groups=mesh['grp'=4,'row'=8] {'row'}, use_global_device_ids=true, to_apply=%region_3.0 | all-reduce | flops 256 | bytes 2048 | tf_op jit(solution)/shard_map/psum | solution.py:46
  74.3 5.7 psum.29
  79.9 0.9 fusion.36
  80.9 59.6 %reduce-scatter.3.cloned.1.call-done = f32[32,256]{1,0:T(8,128)} async-done(((f32[256,256]{1,0:T(8,128)}), f32[32,256]{1,0:T(8,128)}) %reduce-scatter.3.cloned.1.call-update) | async-done | bytes 32784 | tf_op jit(solution)/shard_map/reduce_scatter | solution.py:55
  140.6 2.0 fusion.41
  142.6 129.7 %all-reduce.4.cloned.1.call-done = f32[256,256]{0,1:T(8,128)} async-done(((f32[256,256]{0,1:T(8,128)}), f32[256,256]{0,1:T(8,128)}) %all-reduce.4.cloned.1.call-update) | async-done | bytes 262160 | tf_op jit(solution)/shard_map/psum | solution.py:61
  272.3 1.1 copy.10
  273.4 1.0 fusion.11
  274.4 11.7 %cholesky.130 = f32[128,128]{1,0:T(8,128)S(1)} custom-call(f32[128,128]{1,0:T(8,128)S(1)} %cholesky.194), custom_call_target="Cholesky" | custom-call | tf_op jit(solution)/shard_map/jit(cholesky)/cholesky | solution.py:62
  286.2 9.8 %custom-call.15 = f32[1,128,128]{1,2,0:T(8,128)S(1)} custom-call(f32[1,128,128]{2,1,0:T(8,128)S(1)} %get-tuple-element.53), custom_call_target="InvertDiagBlocksLowerTriangular" | custom-call | tf_op jit(solution)/shard_map/jit(cholesky)/cholesky | solution.py:62
  296.5 11.7 %cholesky.147 = f32[128,128]{1,0:T(8,128)S(1)} custom-call(f32[128,128]{1,0:T(8,128)S(1)} %convolution_subtract_fusion.1), custom_call_target="Cholesky" | custom-call | tf_op jit(solution)/shard_map/jit(cholesky)/cholesky | solution.py:62
  308.2 0.7 compare_reduce_fusion.2
  310.4 4.3 while.4
  310.6 0.6 fusion.64
  311.2 1.4 bitcast_dynamic-update-slice_fusion.4
  312.7 0.6 fusion.64
  313.3 1.4 bitcast_dynamic-update-slice_fusion.4
  314.7 19.7 %custom-call.16 = f32[2,128,128]{1,2,0:T(8,128)S(1)} custom-call(f32[2,128,128]{2,1,0:T(8,128)S(1)} %get-tuple-element.18), custom_call_target="InvertDiagBlocksLowerTriangular" | custom-call | tf_op jit(solution)/shard_map/jit(_solve_triangular)/triangular_solve | solution.py:63
  335.0 5.2 all_gather.21
  340.3 0.9 fusion.35
  341.3 61.2 %reduce-scatter.5.cloned.1.call-done = f32[32,256]{1,0:T(8,128)} async-done(((f32[256,256]{1,0:T(8,128)}), f32[32,256]{1,0:T(8,128)}) %reduce-scatter.5.cloned.1.call-update) | async-done | bytes 32784 | tf_op jit(solution)/shard_map/reduce_scatter | solution.py:55
  402.5 2.0 fusion.42
  404.6 0.5 all-gather.2.cloned.1.call-update
  405.2 0.5 multiply_reduce_fusion
  405.7 128.4 %all-reduce.6.cloned.1.call-done = f32[256,256]{0,1:T(8,128)} async-done(((f32[256,256]{0,1:T(8,128)}), f32[256,256]{0,1:T(8,128)}) %all-reduce.6.cloned.1.call-update) | async-done | bytes 262160 | tf_op jit(solution)/shard_map/psum | solution.py:61
  534.1 1.1 copy.12
  535.1 1.0 fusion.10
  536.1 11.7 %cholesky.164 = f32[128,128]{1,0:T(8,128)S(1)} custom-call(f32[128,128]{1,0:T(8,128)S(1)} %cholesky.197), custom_call_target="Cholesky" | custom-call | tf_op jit(solution)/shard_map/jit(cholesky)/cholesky | solution.py:62
  547.9 9.8 %custom-call.17 = f32[1,128,128]{1,2,0:T(8,128)S(1)} custom-call(f32[1,128,128]{2,1,0:T(8,128)S(1)} %get-tuple-element.49), custom_call_target="InvertDiagBlocksLowerTriangular" | custom-call | tf_op jit(solution)/shard_map/jit(cholesky)/cholesky | solution.py:62
  558.2 11.7 %cholesky.181 = f32[128,128]{1,0:T(8,128)S(1)} custom-call(f32[128,128]{1,0:T(8,128)S(1)} %convolution_subtract_fusion), custom_call_target="Cholesky" | custom-call | tf_op jit(solution)/shard_map/jit(cholesky)/cholesky | solution.py:62
  569.9 0.6 compare_reduce_fusion.1
  570.6 0.6 compare_reduce_fusion
  572.6 4.2 while.5
  572.8 0.6 fusion.65
  573.4 1.4 bitcast_dynamic-update-slice_fusion.5
  574.8 0.6 fusion.65
  575.4 1.4 bitcast_dynamic-update-slice_fusion.5
  576.8 19.7 %custom-call.18 = f32[2,128,128]{1,2,0:T(8,128)S(1)} custom-call(f32[2,128,128]{2,1,0:T(8,128)S(1)} %get-tuple-element.19), custom_call_target="InvertDiagBlocksLowerTriangular" | custom-call | tf_op jit(solution)/shard_map/jit(_solve_triangular)/triangular_solve | solution.py:63
  596.4 2.3 gather_fusion
  599.4 0.6 divide_convert_fusion
  600.0 68.2 %all_gather.23 = bf16[1024,256]{1,0:T(8,128)(2,1)S(1)} all-gather(bf16[32,256]{1,0:T(8,128)(2,1)S(1)} %get-tuple-element.38), channel_id=1, replica_groups=mesh['grp'=4,'row'=8] {'grp','row'}, dimensions={0}, use_global_device_ids=true | all-gather | bytes 540672 | tf_op jit(solution)/shard_map/all_gather | solution.py:71
  668.2 2.1 multiply_reduce_fusion.1
  670.3 4.3 fusion
  674.6 2.3 divide_multiply_fusion
  (52 shorter events, 3.1 us)
Async XLA Ops:
  7.2 133.4 %reduce-scatter.3.cloned.1.call-start = ((), (), s32[]{:S(2)}) async-start(), calls=%async_computation.2 | async-start | bytes 294912 | tf_op jit(solution)/shard_map/reduce_scatter | solution.py:55
  52.5 352.7 %copy-start = (bf16[1024,1024]{1,0:T(8,128)(2,1)S(1)}, bf16[1024,1024]{1,0:T(8,128)(2,1)}, u32[]{:S(2)}) copy-start(bf16[1024,1024]{1,0:T(8,128)(2,1)} %param.8) | copy-start | bytes 6291460
  80.9 191.5 %all-reduce.4.cloned.1.call-start = ((), (), s32[]{:S(2)}) async-start(), calls=%async_computation.3 | async-start | bytes 524288 | tf_op jit(solution)/shard_map/psum | solution.py:61
  140.6 193.8 %copy-start.2 = (f32[32,256]{1,0:T(8,128)S(1)}, f32[32,256]{1,0:T(8,128)}, u32[]{:S(2)}) copy-start(f32[32,256]{1,0:T(8,128)} %reduce-scatter.3.cloned.1.call-done) | copy-start | bytes 98308
  142.6 259.9 %reduce-scatter.5.cloned.1.call-start = ((), (), s32[]{:S(2)}) async-start(), calls=%async_computation.4 | async-start | bytes 294912 | tf_op jit(solution)/shard_map/reduce_scatter | solution.py:55
  341.2 192.9 %all-reduce.6.cloned.1.call-start = ((), (), s32[]{:S(2)}) async-start(), calls=%async_computation.5 | async-start | bytes 524288 | tf_op jit(solution)/shard_map/psum | solution.py:61
  402.5 196.3 %copy-start.1 = (f32[32,256]{1,0:T(8,128)S(1)}, f32[32,256]{1,0:T(8,128)}, u32[]{:S(2)}) copy-start(f32[32,256]{1,0:T(8,128)} %reduce-scatter.5.cloned.1.call-done) | copy-start | bytes 98308
  404.5 263.7 %all-gather.2.cloned.1.call-start = ((), (), s32[]{:S(2)}) async-start(), calls=%async_computation.6 | async-start | bytes 2162688 | tf_op jit(solution)/shard_map/all_gather | solution.py:70
Sparse Core Ops, SparseCore 0:
  81.0 59.5 reduce-scatter.2
  146.7 125.6 all-reduce.3
  341.3 61.1 reduce-scatter.4
  408.4 125.5 all-reduce.5
  536.9 56.1 all-gather.1
where the time goes:
time: 684 us; the launch traced here: 683 us
  waiting for transfers between devices  380 us (56%)
  blocking collectives  145 us (21%)
  other arithmetic  114 us (17%)
  between operations  16.7 us (2%)
  matrix products  14.9 us (2%)
  local copies, waits for them, and re-layouts  12.7 us (2%)
    psum x2, waiting for transfers between devices, body(): lax.psum(jnp.dot(image.T, image, precision=lax.Precision.HIGHEST), ('grp'...  258 us
    reduce_scatter x2, waiting for transfers between devices, body(): lax.psum_scatter(jnp.dot(affinity, cross_basis, preferred_element_type=jn...  121 us
    another operation x13, other arithmetic, body(): lower = jnp.linalg.cholesky(gram)  68.6 us
    all_gather x1, blocking collectives, body(): lax.all_gather(spectral, ('grp', 'row'), axis=0, tiled=True)  68.2 us
    another operation x5, other arithmetic, body(): ortho = jax.scipy.linalg.solve_triangular(lower, image.T, lower=True).T  39.4 us
    all_gather x1, blocking collectives, body(): group_rows = lax.all_gather(landmarks, 'row', axis=0, tiled=True)  32.1 us
    psum x1, blocking collectives, body(): group_degree = lax.psum(jnp.sum(land_kernel, axis=1), 'row')  21.4 us
  transfers between devices with their start and end apart: 5, of which 4 were waited for; matrix products, arithmetic and copies ran while one was open for 9% of the time, Pallas kernels for 0%

commit v1 on v0

--- a/solution.py
+++ b/solution.py
@@ -68,7 +68,12 @@
     point_sq = squared_rows(points)
     numer_part, degree_part = point_terms(
         lax.all_gather(landmarks, ("grp", "row"), axis=0, tiled=True),
-        lax.all_gather(spectral, ("grp", "row"), axis=0, tiled=True),
+        jnp.concatenate(
+            lax.all_to_all(
+                jnp.stack([spectral] * lax.axis_size(("grp", "row"))), ("grp", "row"), 0, 0
+            ),
+            axis=0,
+        ),
         points,
         point_sq,
     )

time: 684 us -> 633 us (0.925)
  blocking collectives: 145 us -> 77.1 us
  waiting for transfers between devices: 380 us -> 388 us
    all_gather x1 -> x0, blocking collectives: 68.2 us -> none  [body(): lax.all_gather(spectral, ('grp', 'row'), axis=0, tiled=True)]
    all_to_all x0 -> x1, waiting for transfers between devices: none -> 7.47 us  [body(): lax.all_to_all(jnp.stack([spectral] * lax.axis_size(('grp', 'row'))), ('g...]
  transfers between devices with their start and end apart: 5 -> 6, of which waited for: 4 -> 5; matrix products, arithmetic and copies ran while one was open for 9% -> 12% of each run, Pallas kernels for 0% -> 0%
where the time goes in v1:
time: 633 us; the launch traced here: 632 us
  waiting for transfers between devices  388 us (61%)
  other arithmetic  114 us (18%)
  blocking collectives  77.1 us (12%)
  matrix products  18.8 us (3%)
  between operations  16.8 us (3%)
  local copies, waits for them, and re-layouts  13.7 us (2%)
    psum x2, waiting for transfers between devices, body(): lax.psum(jnp.dot(image.T, image, precision=lax.Precision.HIGHEST), ('grp'...  259 us
    reduce_scatter x2, waiting for transfers between devices, body(): lax.psum_scatter(jnp.dot(affinity, cross_basis, preferred_element_type=jn...  121 us
    another operation x13, other arithmetic, body(): lower = jnp.linalg.cholesky(gram)  68.7 us
    another operation x5, other arithmetic, body(): ortho = jax.scipy.linalg.solve_triangular(lower, image.T, lower=True).T  39.4 us
    all_gather x1, blocking collectives, body(): group_rows = lax.all_gather(landmarks, 'row', axis=0, tiled=True)  32.1 us
    psum x1, blocking collectives, body(): group_degree = lax.psum(jnp.sum(land_kernel, axis=1), 'row')  21.2 us
  transfers between devices with their start and end apart: 6, of which 5 were waited for; matrix products, arithmetic and copies ran while one was open for 12% of the time, Pallas kernels for 0%

profile of v1, /device:TPU:0, one launch (start us, length us, event | category | flops | bytes accessed | tf_op | source)
XLA Modules:
  0.0 631.9 jit_solution(7932173201342315546)
XLA Ops:
  7.2 7.5 %all_gather.16 = bf16[128,1024]{1,0:T(8,128)(2,1)S(1)} all-gather(bf16[32,1024]{1,0:T(8,128)(2,1)} %param.6), channel_id=1, replica_groups=mesh['grp'=4,'row'=8] {'grp'}, dimensions={0}, use_global_device_ids=true | all-gather | bytes 327680 | tf_op jit(solution)/shard_map/all_gather | solution.py:44
  14.7 32.1 %all_gather.15 = bf16[256,1024]{1,0:T(8,128)(2,1)S(1)} all-gather(bf16[32,1024]{1,0:T(8,128)(2,1)} %param.6), channel_id=1, replica_groups=mesh['grp'=4,'row'=8] {'row'}, dimensions={0}, use_global_device_ids=true | all-gather | bytes 589824 | tf_op jit(solution)/shard_map/all_gather | solution.py:43
  46.7 5.4 all_gather.17
  52.9 21.2 %psum.28 = f32[256]{0:T(256)S(1)} all-reduce(f32[256]{0:T(256)S(1)} %get-tuple-element.20), channel_id=1, replica_groups=mesh['grp'=4,'row'=8] {'row'}, use_global_device_ids=true, to_apply=%region_3.0 | all-reduce | flops 256 | bytes 2048 | tf_op jit(solution)/shard_map/psum | solution.py:46
  74.1 5.7 psum.29
  79.8 0.9 fusion.36
  80.8 59.6 %reduce-scatter.3.cloned.1.call-done = f32[32,256]{1,0:T(8,128)} async-done(((f32[256,256]{1,0:T(8,128)}), f32[32,256]{1,0:T(8,128)}) %reduce-scatter.3.cloned.1.call-update) | async-done | bytes 32784 | tf_op jit(solution)/shard_map/reduce_scatter | solution.py:55
  140.4 2.0 fusion.41
  142.5 129.7 %all-reduce.4.cloned.1.call-done = f32[256,256]{0,1:T(8,128)} async-done(((f32[256,256]{0,1:T(8,128)}), f32[256,256]{0,1:T(8,128)}) %all-reduce.4.cloned.1.call-update) | async-done | bytes 262160 | tf_op jit(solution)/shard_map/psum | solution.py:61
  272.2 1.1 copy.10
  273.3 1.0 fusion.11
  274.3 11.7 %cholesky.130 = f32[128,128]{1,0:T(8,128)S(1)} custom-call(f32[128,128]{1,0:T(8,128)S(1)} %cholesky.194), custom_call_target="Cholesky" | custom-call | tf_op jit(solution)/shard_map/jit(cholesky)/cholesky | solution.py:62
  286.1 9.8 %custom-call.15 = f32[1,128,128]{1,2,0:T(8,128)S(1)} custom-call(f32[1,128,128]{2,1,0:T(8,128)S(1)} %get-tuple-element.53), custom_call_target="InvertDiagBlocksLowerTriangular" | custom-call | tf_op jit(solution)/shard_map/jit(cholesky)/cholesky | solution.py:62
  296.4 11.7 %cholesky.147 = f32[128,128]{1,0:T(8,128)S(1)} custom-call(f32[128,128]{1,0:T(8,128)S(1)} %convolution_subtract_fusion.1), custom_call_target="Cholesky" | custom-call | tf_op jit(solution)/shard_map/jit(cholesky)/cholesky | solution.py:62
  308.2 0.7 compare_reduce_fusion.2
  310.4 4.3 while.4
  310.6 0.6 fusion.64
  311.2 1.4 bitcast_dynamic-update-slice_fusion.4
  312.6 0.6 fusion.64
  313.2 1.4 bitcast_dynamic-update-slice_fusion.4
  314.6 19.7 %custom-call.16 = f32[2,128,128]{1,2,0:T(8,128)S(1)} custom-call(f32[2,128,128]{2,1,0:T(8,128)S(1)} %get-tuple-element.18), custom_call_target="InvertDiagBlocksLowerTriangular" | custom-call | tf_op jit(solution)/shard_map/jit(_solve_triangular)/triangular_solve | solution.py:63
  334.9 5.2 all_gather.18
  340.2 0.9 fusion.35
  341.2 61.2 %reduce-scatter.5.cloned.1.call-done = f32[32,256]{1,0:T(8,128)} async-done(((f32[256,256]{1,0:T(8,128)}), f32[32,256]{1,0:T(8,128)}) %reduce-scatter.5.cloned.1.call-update) | async-done | bytes 32784 | tf_op jit(solution)/shard_map/reduce_scatter | solution.py:55
  402.4 2.0 fusion.42
  404.5 0.5 all-gather.2.cloned.1.call-update
  405.1 128.9 %all-reduce.6.cloned.1.call-done = f32[256,256]{0,1:T(8,128)} async-done(((f32[256,256]{0,1:T(8,128)}), f32[256,256]{0,1:T(8,128)}) %all-reduce.6.cloned.1.call-update) | async-done | bytes 262160 | tf_op jit(solution)/shard_map/psum | solution.py:61
  534.0 1.1 copy.12
  535.1 1.0 fusion.10
  536.1 11.7 %cholesky.164 = f32[128,128]{1,0:T(8,128)S(1)} custom-call(f32[128,128]{1,0:T(8,128)S(1)} %cholesky.197), custom_call_target="Cholesky" | custom-call | tf_op jit(solution)/shard_map/jit(cholesky)/cholesky | solution.py:62
  547.8 9.8 %custom-call.17 = f32[1,128,128]{1,2,0:T(8,128)S(1)} custom-call(f32[1,128,128]{2,1,0:T(8,128)S(1)} %get-tuple-element.49), custom_call_target="InvertDiagBlocksLowerTriangular" | custom-call | tf_op jit(solution)/shard_map/jit(cholesky)/cholesky | solution.py:62
  558.2 11.7 %cholesky.181 = f32[128,128]{1,0:T(8,128)S(1)} custom-call(f32[128,128]{1,0:T(8,128)S(1)} %convolution_subtract_fusion), custom_call_target="Cholesky" | custom-call | tf_op jit(solution)/shard_map/jit(cholesky)/cholesky | solution.py:62
  569.9 0.6 compare_reduce_fusion.1
  570.6 0.7 compare_reduce_fusion
  572.7 4.3 while.5
  572.9 0.6 fusion.65
  573.5 1.4 bitcast_dynamic-update-slice_fusion.5
  575.0 0.6 fusion.65
  575.6 1.4 bitcast_dynamic-update-slice_fusion.5
  577.0 19.7 %custom-call.18 = f32[2,128,128]{1,2,0:T(8,128)S(1)} custom-call(f32[2,128,128]{2,1,0:T(8,128)S(1)} %get-tuple-element.19), custom_call_target="InvertDiagBlocksLowerTriangular" | custom-call | tf_op jit(solution)/shard_map/jit(_solve_triangular)/triangular_solve | solution.py:63
  596.7 2.3 gather_fusion
  599.6 0.6 divide_convert_fusion
  600.3 0.9 stack.2
  601.1 3.7 all-to-all-start
  605.3 2.1 multiply_reduce_fusion.1
  607.4 6.2 fusion
  613.5 7.5 %all-to-all-done = bf16[32,32,256]{2,1,0:T(8,128)(2,1)S(1)} async-done(((bf16[32,32,256]{2,1,0:T(8,128)(2,1)}), bf16[32,32,256]{2,1,0:T(8,128)(2,1)S(1)}, u32[]{:S(2)}, u32[]{:S(2)}) %all-to-all-start) | async-done | bytes 524320 | tf_op jit(solution)/shard_map/all_to_all | solution.py:72
  621.0 4.4 divide_multiply_fusion
  (54 shorter events, 4.0 us)
Async XLA Ops:
  7.2 133.3 %reduce-scatter.3.cloned.1.call-start = ((), (), s32[]{:S(2)}) async-start(), calls=%async_computation.3 | async-start | bytes 294912 | tf_op jit(solution)/shard_map/reduce_scatter | solution.py:55
  80.7 191.5 %all-reduce.4.cloned.1.call-start = ((), (), s32[]{:S(2)}) async-start(), calls=%async_computation.4 | async-start | bytes 524288 | tf_op jit(solution)/shard_map/psum | solution.py:61
  140.4 193.9 %copy-start.2 = (f32[32,256]{1,0:T(8,128)S(1)}, f32[32,256]{1,0:T(8,128)}, u32[]{:S(2)}) copy-start(f32[32,256]{1,0:T(8,128)} %reduce-scatter.3.cloned.1.call-done) | copy-start | bytes 98308
  142.4 260.0 %reduce-scatter.5.cloned.1.call-start = ((), (), s32[]{:S(2)}) async-start(), calls=%async_computation.5 | async-start | bytes 294912 | tf_op jit(solution)/shard_map/reduce_scatter | solution.py:55
  341.1 263.7 %copy-start = (bf16[1024,1024]{1,0:T(8,128)(2,1)S(1)}, bf16[1024,1024]{1,0:T(8,128)(2,1)}, u32[]{:S(2)}) copy-start(bf16[1024,1024]{1,0:T(8,128)(2,1)} %param.8) | copy-start | bytes 6291460
  341.1 192.9 %all-reduce.6.cloned.1.call-start = ((), (), s32[]{:S(2)}) async-start(), calls=%async_computation.6 | async-start | bytes 524288 | tf_op jit(solution)/shard_map/psum | solution.py:61
  402.4 196.6 %copy-start.1 = (f32[32,256]{1,0:T(8,128)S(1)}, f32[32,256]{1,0:T(8,128)}, u32[]{:S(2)}) copy-start(f32[32,256]{1,0:T(8,128)} %reduce-scatter.5.cloned.1.call-done) | copy-start | bytes 98308
  404.4 200.9 %all-gather.2.cloned.1.call-start = ((), (), s32[]{:S(2)}) async-start(), calls=%async_computation.7 | async-start | bytes 2162688 | tf_op jit(solution)/shard_map/all_gather | solution.py:70
  601.1 19.9 %all-to-all-start = ((bf16[32,32,256]{2,1,0:T(8,128)(2,1)}), bf16[32,32,256]{2,1,0:T(8,128)(2,1)S(1)}, u32[]{:S(2)}, u32[]{:S(2)}) async-start(bf16[32,32,256]{2,1,0:T(8,128)(2,1)} %stack.2), calls=%async_computation.2 | async-start | bytes 1048576 | tf_op jit(solution)/shard_map/all_to_all | solution.py:72
Sparse Core Ops, SparseCore 0:
  80.9 59.5 reduce-scatter.2
  146.5 125.6 all-reduce.3
  341.2 61.1 reduce-scatter.4
  408.4 125.5 all-reduce.5
  536.8 56.2 all-gather.1
